TPU v7x, 32 devices: a whole 2x2x4 slice. The times are simulated.
32 devices in a mesh: group: 2 (over y), swap: 8 (over z, x), image: 2 (over core).
Axes of the slice: x: 2, y: 2, z: 4, core: 2. Of those that a mesh axis runs over, the one named last changes fastest.
Arguments:
- images_in: bfloat16 [16, 1536, 4096], P(('group', 'image'), 'swap'), parts along dimension 0, may hold values from -6 to 6
- kernel: bfloat16 [1536, 49], P('swap'), may hold values from -1.75 to 1.75
- conv_bias: float32 [1536], P('swap'), may hold values from -1 to 1
- norm_gain: float32 [1536], replicated, may hold values from 0.1 to 1.9
- norm_shift: float32 [1536], replicated, may hold values from -0.5 to 0.5
- fp8_weight: bfloat16 [1536, 6144], P('swap', 'image'), may hold values from -1.875 to 1.875, as said below
- block_scale: int32 [1536, 48], P('swap', 'image'), may hold values from -7 to -5
- adapter_a: bfloat16 [1536, 32], replicated, may hold values from -0.15625 to 0.15625
- adapter_b: bfloat16 [32, 6144], P(None, 'image'), may hold values from -0.25 to 0.25
- cotangent: bfloat16 [16, 4096, 6144], P('group', 'swap', 'image'), parts along dimension 0, may hold values from -0.05 to 0.05
Outputs:
- grad_a: float32 [3072, 32], P('group'), parts along dimension 0
- grad_b: float32 [64, 6144], P('group', 'image'), parts along dimension 0
There are 2 independent parts, one for each index of `group`. A program takes and returns all parts, laid end to end along the dimension named above; an argument that names none is the same for every part. Nothing has to cross between parts.
Inputs may be any that keep to these rules, and one draw needn't show every extreme that they name: `fp8_weight`: each entry is a value of the E4M3 format: a sign times 2 to an integer power times 1 + k / 8 for an integer k of 0 to 7. `block_scale`: the entry at [c, j] is the exponent of the scale of hidden units 128 * j to 128 * j + 127 of weight row c.
All inputs are finite; a program needn't handle non-finite values.
Results may differ from a plain program's by a relative error of at most 0.00055.
The roundings to bfloat16 on the way count: a program that leaves them out, or rounds other values in their place, can miss the bound.
Values may be sent and summed in bfloat16 or wider, within the bound.
A program may use at most 192 MiB of HBM per device.

v0:
```python
import jax
import jax.numpy as jnp
from jax import lax
from jax.sharding import PartitionSpec as P

KS = 7
W = 64
adapter_scale = 2.0
norm_eps = 1e-06


def power_table(scales):
    factor = jnp.zeros(scales.shape, jnp.float32)
    for exponent in range(-12, 4):
        factor = factor + jnp.where(
            scales == exponent, jnp.float32(2.0**exponent), jnp.float32(0.0)
        )
    return factor


def decode(weight, scales):
    row_count = weight.shape[0]
    groups = scales.shape[1]
    blocks = (
        weight.reshape(row_count, groups, -1).astype(jnp.float32) * power_table(scales)[:, :, None]
    )
    return blocks.reshape(row_count, -1).astype(jnp.bfloat16)


def gelu_slope(pre_act):
    cumulative = 0.5 * (1.0 + jax.scipy.special.erf(pre_act * 0.7071067811865476))
    density = jnp.exp(-0.5 * pre_act * pre_act) * 0.3989422804014327
    return cumulative + pre_act * density


def depthwise(images, kernel, conv_bias, map_width):
    batch, channels, pixels = images.shape
    maps = images.reshape(batch, channels, pixels // map_width, map_width)
    taps = kernel.reshape(channels, 1, KS, KS)
    half_span = KS // 2
    summed = lax.conv_general_dilated(
        maps,
        taps,
        (1, 1),
        ((half_span, half_span), (half_span, half_span)),
        dimension_numbers=("NCHW", "OIHW", "NCHW"),
        feature_group_count=channels,
        preferred_element_type=jnp.float32,
    )
    summed = summed.reshape(batch, channels, pixels)
    return summed + conv_bias[None, :, None]


def shards(
    images_in,
    kernel,
    conv_bias,
    norm_gain,
    norm_shift,
    fp8_weight,
    block_scale,
    adapter_a,
    adapter_b,
    cotangent,
):
    conv = depthwise(images_in, kernel, conv_bias, W).astype(jnp.bfloat16)
    values = lax.all_to_all(conv, "swap", split_axis=2, concat_axis=1, tiled=True).astype(
        jnp.float32
    )
    average = jnp.mean(values, axis=1, keepdims=True)
    centred = values - average
    variance = jnp.mean(centred * centred, axis=1, keepdims=True)
    scaled = (
        centred * lax.rsqrt(variance + norm_eps) * norm_gain[None, :, None]
        + norm_shift[None, :, None]
    )
    normed = jnp.swapaxes(scaled, 1, 2).astype(jnp.bfloat16)
    own_rows = normed.reshape(-1, normed.shape[2])
    tokens = lax.all_gather(own_rows, "image", axis=0, tiled=True)
    zero_start = jnp.zeros((tokens.shape[0], fp8_weight.shape[1]), jnp.float32)
    local_weight = decode(fp8_weight, block_scale)
    shard_rows = lax.all_gather(local_weight, "swap", axis=0, tiled=True)
    columns = lax.slice_in_dim(tokens, 0, shard_rows.shape[0], axis=1)
    frozen = zero_start + jnp.dot(columns, shard_rows, preferred_element_type=jnp.float32)
    low_rank = jnp.dot(tokens, adapter_a, preferred_element_type=jnp.float32).astype(jnp.bfloat16)
    pre_act = frozen + adapter_scale * jnp.dot(
        low_rank, adapter_b, preferred_element_type=jnp.float32
    )
    upstream = cotangent.reshape(-1, cotangent.shape[2])
    grad_pre = (upstream.astype(jnp.float32) * gelu_slope(pre_act)).astype(jnp.bfloat16)
    grad_b_local = adapter_scale * jnp.dot(low_rank.T, grad_pre, preferred_element_type=jnp.float32)
    partial_back = jnp.dot(grad_pre, adapter_b.T, preferred_element_type=jnp.float32)
    contract = (((0,), (0,)), ((), ()))
    tokens_wide = tokens.astype(jnp.float32)
    summed_back = lax.psum(partial_back, "image")
    grad_a_local = adapter_scale * lax.dot_general(
        tokens_wide,
        summed_back,
        contract,
        precision=lax.Precision.HIGHEST,
        preferred_element_type=jnp.float32,
    )
    grad_a, grad_b = lax.psum((grad_a_local, grad_b_local), "swap")
    return (grad_a, grad_b)


def solution(mesh):
    placed = (
        P(("group", "image"), "swap", None),
        P("swap", None),
        P("swap"),
        P(),
        P(),
        P("swap", "image"),
        P("swap", "image"),
        P(),
        P(None, "image"),
        P("group", "swap", "image"),
    )
    return jax.shard_map(
        shards,
        mesh=mesh,
        in_specs=placed,
        out_specs=(P("group", None), P("group", "image")),
        check_vma=False,
    )
```

profile of v0, /device:TPU:0, one launch (start us, length us, event | category | flops | bytes accessed | tf_op | source)
XLA Modules:
  0.0 837.5 jit_solution(14557225846373415734)
XLA Ops:
  8.1 10.6 %copy.43 = bf16[4,192,4096]{1,2,0:T(8,128)(2,1)} copy(bf16[4,192,4096]{2,1,0:T(8,128)(2,1)} %param.10) | data formatting | bytes 12582912 | tf_op args[0]
  18.7 11.5 %copy.54 = bf16[192,64,4,64]{0,1,3,2:T(8,128)(2,1)} copy(bf16[192,64,4,64]{0,3,1,2:T(8,128)(2,1)} %bitcast.75) | data formatting | bytes 12582912
  30.2 10.0 %pad.clone = bf16[192,64,4,72]{0,1,3,2:T(8,128)(2,1)} pad(bf16[192,64,4,64]{0,1,3,2:T(8,128)(2,1)} %copy.54, bf16[]{:T(256)} %constant.37), padding=0_0x0_0x0_0x3_5 | pad | bytes 13369346 | tf_op jit(solution)/shard_map/reshape | solution.py:38
  40.2 3.4 slice.2
  43.7 1.9 copy-done.2
  45.5 4.2 fusion.8
  49.7 95.5 %broadcast_select_fusion = f32[64,32,9,192]{3,1,2,0:T(8,128)S(1)} fusion(pred[32,9]{0,1:T(8,128)(4,1)S(1)} %copy-done.9, bf16[192,1,7,7]{0,1,3,2:T(2,128)(2,1)S(1)} %reshape.62, bf16[192,64,4,8,15]{0,1,4,3,2:T(8,128)(2,1)S(1)} %fusion.8), kind=kOutput, calls=%fused_computation.23 | convolution fusion | flops 341065728 | bytes 25971360 | tf_op jit(solution)/shard_map/conv_general_dilated | solution.py:41
  145.3 20.1 %copy.47 = f32[64,32,9,192]{3,0,2,1:T(8,128)S(1)} copy(f32[64,32,9,192]{3,1,2,0:T(8,128)S(1)} %broadcast_select_fusion) | data formatting | bytes 28311552 | tf_op jit(solution)/shard_map/conv_general_dilated | solution.py:41
  165.4 2.0 slice_bitcast_fusion
  167.4 17.9 %copy.48 = f32[4,192,64,64]{1,3,2,0:T(8,128)S(1)} copy(f32[4,192,64,64]{1,2,3,0:T(8,128)S(1)} %slice_bitcast_fusion) | data formatting | bytes 25165824 | tf_op jit(solution)/shard_map/conv_general_dilated | solution.py:41
  185.3 2.5 fusion.7
  187.9 31.9 %copy.49 = bf16[4,192,4096]{1,0,2:T(4,128)(2,1)S(1)} copy(bf16[4,192,4096]{1,2,0:T(8,128)(2,1)S(1)} %fusion.7) | data formatting | bytes 12582912 | tf_op jit(solution)/shard_map/convert_element_type | solution.py:66
  219.8 190.2 %all_to_all.4 = bf16[4,192,4096]{1,0,2:T(4,128)(2,1)} all-to-all(bf16[4,192,4096]{1,0,2:T(4,128)(2,1)S(1)} %copy.49), channel_id=1, replica_groups=mesh['group'=2,'swap'=8,'image'=2] {'swap'}, dimensions={2} | all-to-all | bytes 12582912 | tf_op jit(solution)/shard_map/all_to_all | solution.py:67
  410.0 13.5 %copy.50 = bf16[4,192,4096]{2,1,0:T(8,128)(2,1)} copy(bf16[4,192,4096]{1,0,2:T(4,128)(2,1)} %all_to_all.4) | data formatting | bytes 12582912 | tf_op jit(solution)/shard_map/all_to_all | solution.py:67
  423.6 9.1 %copy.55 = f32[96,8,8,512]{3,2,1,0:T(8,128)S(1)} copy(bf16[96,8,8,512]{3,1,2,0:T(8,128)(2,1)} %bitcast.77) | data formatting | bytes 18874368
  433.6 3.5 copy-done.1
  438.7 10.6 %bitcast_bitcast_fusion = f32[4,8,192,512]{3,1,2,0:T(8,128)} fusion(f32[4,192,8,512]{3,2,1,0:T(8,128)} %bitcast.71), kind=kLoop, calls=%fused_computation.16 | loop fusion | bytes 25165824 | tf_op jit(solution)/shard_map/convert_element_type | solution.py:67
  449.4 16.7 %copy.51 = f32[4,8,192,512]{3,2,1,0:T(8,128)} copy(f32[4,8,192,512]{3,1,2,0:T(8,128)} %bitcast_bitcast_fusion) | data formatting | bytes 25165824 | tf_op jit(solution)/shard_map/convert_element_type | solution.py:67
  466.1 9.0 %fusion.15 = bf16[4,1536,512]{2,1,0:T(8,128)(2,1)} fusion(f32[4,8,192,512]{3,2,1,0:T(8,128)} %copy.51, f32[1536]{0:T(1024)S(1)} %copy-done.6, f32[1536]{0:T(1024)S(1)} %copy-done.7, f32[4,512]{1,0:T(4,128)S(1)} %add_rsqrt_fusion, f32[4,512]{1,0:T(4,128)S(1)} %broadcast_multiply_fusion), kind=kLoop, calls=%fused_computation.21 | loop fusion | flops 15728640 | bytes 18903040 | tf_op jit(solution)/shard_map/convert_element_type | solution.py:77
  475.1 8.7 %copy.52 = bf16[4,512,1536]{2,1,0:T(8,128)(2,1)} copy(bf16[4,512,1536]{1,2,0:T(8,128)(2,1)} %bitcast.78) | data formatting | bytes 12582912 | tf_op jit(solution)/shard_map/convert_element_type | solution.py:77
  484.7 1.6 fusion.18
  486.4 21.3 %all-gather.3.cloned.1.call-done = bf16[4096,1536]{1,0:T(8,128)(2,1)} async-done(((bf16[2048,1536]{1,0:T(8,128)(2,1)}), bf16[4096,1536]{1,0:T(8,128)(2,1)}) %all-gather.3.cloned.1.call-update) | async-done | bytes 12582928 | tf_op jit(solution)/shard_map/all_gather | solution.py:79
  507.7 8.3 convolution_convert_fusion
  516.0 20.1 %fusion.20 = f32[4096,3072]{1,0:T(8,128)} fusion(bf16[4096,32]{0,1:T(8,128)(2,1)S(1)} %convolution_convert_fusion, bf16[32,3072]{1,0:T(8,128)(2,1)S(1)} %copy-done), kind=kOutput, calls=%fused_computation.33 | convolution fusion | flops 805306368 | bytes 50790400 | tf_op jit(solution)/shard_map/dot_general | solution.py:86
  536.2 112.2 %all-gather.5.cloned.1.call-done = bf16[1536,3072]{1,0:T(8,128)(2,1)} async-done(((bf16[192,3072]{1,0:T(8,128)(2,1)}), bf16[1536,3072]{1,0:T(8,128)(2,1)}) %all-gather.5.cloned.1.call-update) | async-done | bytes 9437200 | tf_op jit(solution)/shard_map/all_gather | solution.py:82
  648.3 64.7 %fusion.5 = bf16[4096,3072]{1,0:T(8,128)(2,1)} fusion(bf16[4096,3072]{1,0:T(8,128)(2,1)} %bitcast.80, f32[4096,3072]{1,0:T(8,128)} %fusion.20, bf16[4096,1536]{1,0:T(8,128)(2,1)} %all-gather.3.cloned.1.call-done, bf16[1536,3072]{1,0:T(8,128)(2,1)} %all-gather.5.cloned.1.call-done), kind=kOutput, calls=%fused_computation.6 | convolution fusion | flops 38818283520 | bytes 122683392 | tf_op jit(solution)/shard_map/dot_general | solution.py:84
  713.0 12.9 %fusion.21 = f32[4096,32]{0,1:T(8,128)} fusion(bf16[4096,3072]{1,0:T(8,128)(2,1)} %fusion.5, bf16[32,3072]{1,0:T(8,128)(2,1)S(1)} %copy-done), kind=kOutput, calls=%fused_computation.34 | convolution fusion | flops 805306368 | bytes 25886720 | tf_op jit(solution)/shard_map/dot_general | solution.py:92
  726.0 11.7 %convolution_multiply_fusion = f32[32,3072]{1,0:T(8,128)} fusion(bf16[4096,32]{0,1:T(8,128)(2,1)S(1)} %convolution_convert_fusion, bf16[4096,3072]{1,0:T(8,128)(2,1)} %fusion.5), kind=kOutput, calls=%fused_computation.25 | convolution fusion | flops 805404672 | bytes 25821184 | tf_op jit(solution)/shard_map/dot_general | solution.py:91
  737.7 5.2 all-reduce.4.cloned.1.call-done
  742.8 9.8 %convolution_multiply_fusion.1 = f32[1536,32]{0,1:T(8,128)} fusion(bf16[4096,1536]{1,0:T(8,128)(2,1)} %all-gather.3.cloned.1.call-done, f32[4096,32]{0,1:T(8,128)} %all-reduce.4.cloned.1.call-done), kind=kOutput, calls=%fused_computation.28 | convolution fusion | flops 2415968256 | bytes 13303808 | tf_op jit(solution)/shard_map/dot_general | solution.py:96
  752.7 74.7 %all-reduce.6.cloned.1.call-done = (f32[1536,32]{0,1:T(8,128)}, f32[32,3072]{1,0:T(8,128)}) async-done(((f32[1536,32]{0,1:T(8,128)}, f32[32,3072]{1,0:T(8,128)}), (f32[1536,32]{0,1:T(8,128)}, f32[32,3072]{1,0:T(8,128)})) %all-reduce.6.cloned.1.call-update) | async-done | bytes 589840 | tf_op jit(solution)/shard_map/psum | solution.py:103
  829.0 1.8 copy.68
  (35 shorter events, 6.2 us)
Async XLA Ops:
  7.2 508.9 %copy-start = (bf16[32,3072]{1,0:T(8,128)(2,1)S(1)}, bf16[32,3072]{1,0:T(8,128)(2,1)}, u32[]{:S(2)}) copy-start(bf16[32,3072]{1,0:T(8,128)(2,1)} %param.18) | copy-start | bytes 589828
  7.2 500.5 %all-gather.3.cloned.1.call-start = ((), (), s32[]{:S(2)}) async-start(), calls=%async_computation.1 | async-start | bytes 18874368 | tf_op jit(solution)/shard_map/all_gather | solution.py:79
  40.2 5.3 copy-start.2
  45.5 4.2 copy-start.9
  167.4 17.9 %copy-start.8 = (f32[192]{0:T(256)S(1)}, f32[192]{0:T(256)}, u32[]{:S(2)}) copy-start(f32[192]{0:T(256)} %param.12) | copy-start | bytes 2308
  432.6 4.5 copy-start.1
  449.4 16.8 %copy-start.6 = (f32[1536]{0:T(1024)S(1)}, f32[1536]{0:T(1024)}, u32[]{:S(2)}) copy-start(f32[1536]{0:T(1024)} %param.14) | copy-start | bytes 18436
  449.4 16.8 %copy-start.7 = (f32[1536]{0:T(1024)S(1)}, f32[1536]{0:T(1024)}, u32[]{:S(2)}) copy-start(f32[1536]{0:T(1024)} %param.13) | copy-start | bytes 18436
  466.1 17.8 %copy-start.5 = (s32[192,24]{0,1:T(8,128)S(1)}, s32[192,24]{0,1:T(8,128)}, u32[]{:S(2)}) copy-start(s32[192,24]{0,1:T(8,128)} %param.16) | copy-start | bytes 55300
  466.1 18.6 %copy-start.3 = (bf16[192,3072]{1,0:T(8,128)(2,1)S(1)}, bf16[192,3072]{1,0:T(8,128)(2,1)}, u32[]{:S(2)}) copy-start(bf16[192,3072]{1,0:T(8,128)(2,1)} %param.15) | copy-start | bytes 3538948
  475.1 32.6 %copy-start.4 = (bf16[1536,32]{0,1:T(8,128)(2,1)S(1)}, bf16[1536,32]{0,1:T(8,128)(2,1)}, u32[]{:S(2)}) copy-start(bf16[1536,32]{0,1:T(8,128)(2,1)} %param.17) | copy-start | bytes 294916
  483.8 164.5 %all-gather.5.cloned.1.call-start = ((), (), s32[]{:S(2)}) async-start(), calls=%async_computation.2 | async-start | bytes 10616832 | tf_op jit(solution)/shard_map/all_gather | solution.py:82
  486.4 256.5 %all-reduce.4.cloned.1.call-start = ((), (), s32[]{:S(2)}) async-start(), calls=%async_computation.3 | async-start | bytes 1048576 | tf_op jit(solution)/shard_map/psum | solution.py:95
  725.9 101.4 %all-reduce.6.cloned.1.call-start = ((), (), s32[]{:S(2)}) async-start(), calls=%async_computation.4 | async-start | bytes 1179648 | tf_op jit(solution)/shard_map/psum | solution.py:103
Sparse Core Ops, SparseCore 0:
  484.0 23.7 all-gather.2
  509.9 138.3 all-gather.4
  726.0 16.7 all-reduce.3
  752.8 74.5 all-reduce.5
where the time goes:
time: 845 us; the launch traced here: 837 us
  matrix products  223 us (26%)
  waiting for transfers between devices  213 us (25%)
  blocking collectives  190 us (22%)
  local copies, waits for them, and re-layouts  176 us (21%)
  other arithmetic  20 us (2%)
  between operations  14.2 us (2%)
    all_to_all x1, blocking collectives, shards(): lax.all_to_all(conv, 'swap', split_axis=2, concat_axis=1, tiled=True)  190 us
    all_gather x1, waiting for transfers between devices, shards(): shard_rows = lax.all_gather(local_weight, 'swap', axis=0, tiled=True)  112 us
    conv_general_dilated x1, matrix products, depthwise(): lax.conv_general_dilated(maps, taps, (1, 1), ((half_span, half_span), (ha...  95.5 us
    psum x1, waiting for transfers between devices, shards(): grad_a, grad_b = lax.psum((grad_a_local, grad_b_local), 'swap')  74.7 us
    dot_general x1, matrix products, shards(): jnp.dot(columns, shard_rows, preferred_element_type=jnp.float32)  64.7 us
    conv_general_dilated x4, local copies, waits for them, and re-layouts, depthwise(): lax.conv_general_dilated(maps, taps, (1, 1), ((half_span, half_span), (ha...  43.4 us
    unnamed x25, local copies, waits for them, and re-layouts  40 us
    convert_element_type x1, local copies, waits for them, and re-layouts, shards(): conv = depthwise(images_in, kernel, conv_bias, W).astype(jnp.bfloat16)  31.9 us
  transfers between devices with their start and end apart: 4, of which 4 were waited for; matrix products, arithmetic and copies ran while one was open for 5% of the time, Pallas kernels for 0%

commit v1 on v0

--- a/solution.py
+++ b/solution.py
@@ -7,6 +7,36 @@
 W = 64
 adapter_scale = 2.0
 norm_eps = 1e-06
+
+
+def begin_matrix(local_values, axis_tag):
+    base_arr, field_out, piece_next = (
+        lax.axis_size(axis_tag),
+        lax.axis_index(axis_tag),
+        local_values.shape[0],
+    )
+    heap = [(hop_no, (hop_no + 1) % base_arr) for hop_no in range(base_arr)]
+    before = jnp.zeros(
+        (*local_values.shape[:0], base_arr * piece_next, *local_values.shape[1:]),
+        local_values.dtype,
+    )
+    before = lax.dynamic_update_slice_in_dim(before, local_values, field_out * piece_next, axis=0)
+    all_rows = [(hop_no, (hop_no - 1) % base_arr) for hop_no in range(base_arr)]
+    inter = vec_out = local_values
+    src_i = 1
+    outer = base_arr // 2
+    while src_i < outer + 1:
+        inter = lax.ppermute(inter, axis_tag, heap)
+        before = lax.dynamic_update_slice_in_dim(
+            before, inter, (field_out - src_i) % base_arr * piece_next, axis=0
+        )
+        if src_i < base_arr - outer:
+            vec_out = lax.ppermute(vec_out, axis_tag, perm=all_rows)
+            before = lax.dynamic_update_slice_in_dim(
+                before, vec_out, (field_out + src_i) % base_arr * piece_next, axis=0
+            )
+        src_i += 1
+    return before
 
 
 def power_table(scales):
@@ -79,7 +109,7 @@
     tokens = lax.all_gather(own_rows, "image", axis=0, tiled=True)
     zero_start = jnp.zeros((tokens.shape[0], fp8_weight.shape[1]), jnp.float32)
     local_weight = decode(fp8_weight, block_scale)
-    shard_rows = lax.all_gather(local_weight, "swap", axis=0, tiled=True)
+    shard_rows = begin_matrix(local_weight, "swap")
     columns = lax.slice_in_dim(tokens, 0, shard_rows.shape[0], axis=1)
     frozen = zero_start + jnp.dot(columns, shard_rows, preferred_element_type=jnp.float32)
     low_rank = jnp.dot(tokens, adapter_a, preferred_element_type=jnp.float32).astype(jnp.bfloat16)

time: 845 us -> 898 us (1.063)
  waiting for transfers between devices: 213 us -> 235 us
  local copies, waits for them, and re-layouts: 176 us -> 193 us
  starting transfers between devices: 0.16 us -> 17 us
    ppermute x0 -> x7, waiting for transfers between devices: none -> 156 us  [the longest x4 156 us: begin_matrix(): inter = lax.ppermute(inter, axis_tag, heap)]
    all_gather x1 -> x0, waiting for transfers between devices: 112 us -> none  [shards(): shard_rows = lax.all_gather(local_weight, 'swap', axis=0, tiled=True)]
    all_gather x1, waiting for transfers between devices: 21.3 us -> 0.01 us  [shards(): tokens = lax.all_gather(own_rows, 'image', axis=0, tiled=True)]
    ppermute x0 -> x7, starting transfers between devices: none -> 16.7 us  [the longest x4 8.72 us: begin_matrix(): inter = lax.ppermute(inter, axis_tag, heap)]
    dynamic_update_slice x0 -> x7, local copies, waits for them, and re-layouts: none -> 11.7 us  [the longest x4 7.08 us: begin_matrix(): lax.dynamic_update_slice_in_dim(before, inter, (field_out - src_i) % base...]
    unnamed x25 -> x29, local copies, waits for them, and re-layouts: 40 us -> 43.4 us
  transfers between devices with their start and end apart: 4 -> 10, of which waited for: 4 -> 6; matrix products, arithmetic and copies ran while one was open for 5% -> 3% of each run, Pallas kernels for 0% -> 0%
where the time goes in v1:
time: 898 us; the launch traced here: 890 us
  waiting for transfers between devices  235 us (26%)
  matrix products  222 us (25%)
  local copies, waits for them, and re-layouts  193 us (21%)
  blocking collectives  190 us (21%)
  other arithmetic  19 us (2%)
  starting transfers between devices  17 us (2%)
  between operations  14.2 us (2%)
    all_to_all x1, blocking collectives, shards(): lax.all_to_all(conv, 'swap', split_axis=2, concat_axis=1, tiled=True)  190 us
    ppermute x4, waiting for transfers between devices, begin_matrix(): inter = lax.ppermute(inter, axis_tag, heap)  156 us
    conv_general_dilated x1, matrix products, depthwise(): lax.conv_general_dilated(maps, taps, (1, 1), ((half_span, half_span), (ha...  95.5 us
    psum x1, waiting for transfers between devices, shards(): grad_a, grad_b = lax.psum((grad_a_local, grad_b_local), 'swap')  74.7 us
    dot_general x1, matrix products, shards(): jnp.dot(columns, shard_rows, preferred_element_type=jnp.float32)  64.8 us
    unnamed x29, local copies, waits for them, and re-layouts  43.4 us
    conv_general_dilated x4, local copies, waits for them, and re-layouts, depthwise(): lax.conv_general_dilated(maps, taps, (1, 1), ((half_span, half_span), (ha...  43.4 us
    convert_element_type x1, local copies, waits for them, and re-layouts, shards(): conv = depthwise(images_in, kernel, conv_bias, W).astype(jnp.bfloat16)  31.9 us
  transfers between devices with their start and end apart: 10, of which 6 were waited for; matrix products, arithmetic and copies ran while one was open for 3% of the time, Pallas kernels for 0%

profile of v1, /device:TPU:0, one launch (start us, length us, event | category | flops | bytes accessed | tf_op | source)
XLA Modules:
  0.0 890.4 jit_solution(12223512320984296877)
XLA Ops:
  8.1 10.7 %copy.43 = bf16[4,192,4096]{1,2,0:T(8,128)(2,1)} copy(bf16[4,192,4096]{2,1,0:T(8,128)(2,1)} %param.10) | data formatting | bytes 12582912 | tf_op args[0]
  18.7 11.6 %copy.54 = bf16[192,64,4,64]{0,1,3,2:T(8,128)(2,1)} copy(bf16[192,64,4,64]{0,3,1,2:T(8,128)(2,1)} %bitcast.76) | data formatting | bytes 12582912
  30.3 10.0 %pad.clone = bf16[192,64,4,72]{0,1,3,2:T(8,128)(2,1)} pad(bf16[192,64,4,64]{0,1,3,2:T(8,128)(2,1)} %copy.54, bf16[]{:T(256)} %constant.48.clone.1), padding=0_0x0_0x0_0x3_5 | pad | bytes 13369346 | tf_op jit(solution)/shard_map/reshape | solution.py:68
  40.3 3.4 slice.2
  45.6 4.2 fusion.8
  49.8 95.5 %broadcast_select_fusion = f32[64,32,9,192]{3,1,2,0:T(8,128)S(1)} fusion(pred[32,9]{0,1:T(8,128)(4,1)S(1)} %copy-done.11, bf16[192,1,7,7]{0,1,3,2:T(2,128)(2,1)S(1)} %reshape.62, bf16[192,64,4,8,15]{0,1,4,3,2:T(8,128)(2,1)S(1)} %fusion.8), kind=kOutput, calls=%fused_computation.23 | convolution fusion | flops 341065728 | bytes 25971360 | tf_op jit(solution)/shard_map/conv_general_dilated | solution.py:71
  145.3 20.1 %copy.47 = f32[64,32,9,192]{3,0,2,1:T(8,128)S(1)} copy(f32[64,32,9,192]{3,1,2,0:T(8,128)S(1)} %broadcast_select_fusion) | data formatting | bytes 28311552 | tf_op jit(solution)/shard_map/conv_general_dilated | solution.py:71
  167.5 17.9 %copy.48 = f32[4,192,64,64]{1,3,2,0:T(8,128)S(1)} copy(f32[4,192,64,64]{1,2,3,0:T(8,128)S(1)} %slice_bitcast_fusion) | data formatting | bytes 25165824 | tf_op jit(solution)/shard_map/conv_general_dilated | solution.py:71
  185.4 2.5 fusion.7
  188.0 31.9 %copy.49 = bf16[4,192,4096]{1,0,2:T(4,128)(2,1)S(1)} copy(bf16[4,192,4096]{1,2,0:T(8,128)(2,1)S(1)} %fusion.7) | data formatting | bytes 12582912 | tf_op jit(solution)/shard_map/convert_element_type | solution.py:96
  219.8 190.2 %all_to_all.4 = bf16[4,192,4096]{1,0,2:T(4,128)(2,1)} all-to-all(bf16[4,192,4096]{1,0,2:T(4,128)(2,1)S(1)} %copy.49), channel_id=1, replica_groups=mesh['group'=2,'swap'=8,'image'=2] {'swap'}, dimensions={2} | all-to-all | bytes 12582912 | tf_op jit(solution)/shard_map/all_to_all | solution.py:97
  410.1 13.5 %copy.50 = bf16[4,192,4096]{2,1,0:T(8,128)(2,1)} copy(bf16[4,192,4096]{1,0,2:T(4,128)(2,1)} %all_to_all.4) | data formatting | bytes 12582912 | tf_op jit(solution)/shard_map/all_to_all | solution.py:97
  423.6 9.1 %copy.55 = f32[96,8,8,512]{3,2,1,0:T(8,128)S(1)} copy(bf16[96,8,8,512]{3,1,2,0:T(8,128)(2,1)} %bitcast.78) | data formatting | bytes 18874368
  437.8 10.6 %bitcast_bitcast_fusion = f32[4,8,192,512]{3,1,2,0:T(8,128)} fusion(f32[4,192,8,512]{3,2,1,0:T(8,128)} %bitcast.72), kind=kLoop, calls=%fused_computation.16 | loop fusion | bytes 25165824 | tf_op jit(solution)/shard_map/convert_element_type | solution.py:97
  448.4 16.8 %copy.51 = f32[4,8,192,512]{3,2,1,0:T(8,128)} copy(f32[4,8,192,512]{3,1,2,0:T(8,128)} %bitcast_bitcast_fusion) | data formatting | bytes 25165824 | tf_op jit(solution)/shard_map/convert_element_type | solution.py:97
  465.2 8.9 fusion.15
  474.0 8.8 copy.52
  485.6 4.4 copy-done.3
  491.2 3.6 collective-permute-start.1
  494.8 45.4 %collective-permute-done = bf16[192,3072]{1,0:T(8,128)(2,1)S(1)} collective-permute-done((bf16[192,3072]{1,0:T(8,128)(2,1)S(1)}, bf16[192,3072]{1,0:T(8,128)(2,1)S(1)}, u32[]{:S(2)}, u32[]{:S(2)}) %collective-permute-start) | collective-permute-done | bytes 1179680 | tf_op jit(solution)/shard_map/ppermute | solution.py:29
  544.9 47.1 %collective-permute-done.2 = bf16[192,3072]{1,0:T(8,128)(2,1)} collective-permute-done((bf16[192,3072]{1,0:T(8,128)(2,1)S(1)}, bf16[192,3072]{1,0:T(8,128)(2,1)}, u32[]{:S(2)}, u32[]{:S(2)}) %collective-permute-start.2) | collective-permute-done | bytes 1179680 | tf_op jit(solution)/shard_map/ppermute | solution.py:29
  592.0 2.6 collective-permute-start.4
  601.5 42.9 %collective-permute-done.4 = bf16[192,3072]{1,0:T(8,128)(2,1)S(1)} collective-permute-done((bf16[192,3072]{1,0:T(8,128)(2,1)}, bf16[192,3072]{1,0:T(8,128)(2,1)S(1)}, u32[]{:S(2)}, u32[]{:S(2)}) %collective-permute-start.4) | collective-permute-done | bytes 1179680 | tf_op jit(solution)/shard_map/ppermute | solution.py:29
  652.7 20.4 %collective-permute-done.6 = bf16[192,3072]{1,0:T(8,128)(2,1)S(1)} collective-permute-done((bf16[192,3072]{1,0:T(8,128)(2,1)S(1)}, bf16[192,3072]{1,0:T(8,128)(2,1)S(1)}, u32[]{:S(2)}, u32[]{:S(2)}) %collective-permute-start.6) | collective-permute-done | bytes 1179680 | tf_op jit(solution)/shard_map/ppermute | solution.py:29
  674.2 8.3 convolution_convert_fusion
  682.5 19.4 %fusion.21 = f32[4096,3072]{1,0:T(8,128)} fusion(bf16[4096,32]{0,1:T(8,128)(2,1)S(1)} %convolution_convert_fusion, bf16[32,3072]{1,0:T(8,128)(2,1)S(1)} %copy-done), kind=kOutput, calls=%fused_computation.41 | convolution fusion | flops 805306368 | bytes 50790400 | tf_op jit(solution)/shard_map/dot_general | solution.py:116
  701.9 64.8 %fusion.5 = bf16[4096,3072]{1,0:T(8,128)(2,1)} fusion(bf16[4096,3072]{1,0:T(8,128)(2,1)} %bitcast.81, f32[4096,3072]{1,0:T(8,128)} %fusion.21, bf16[4096,1536]{1,0:T(8,128)(2,1)} %all-gather.2.cloned.1.call-done, bf16[1536,3072]{1,0:T(8,128)(2,1)} %constant_dynamic-update-slice_fusion), kind=kOutput, calls=%fused_computation.6 | convolution fusion | flops 38818283520 | bytes 122683392 | tf_op jit(solution)/shard_map/dot_general | solution.py:114
  766.7 12.9 %fusion.22 = f32[4096,32]{0,1:T(8,128)} fusion(bf16[4096,3072]{1,0:T(8,128)(2,1)} %fusion.5, bf16[32,3072]{1,0:T(8,128)(2,1)S(1)} %copy-done), kind=kOutput, calls=%fused_computation.42 | convolution fusion | flops 805306368 | bytes 25886720 | tf_op jit(solution)/shard_map/dot_general | solution.py:122
  779.9 11.5 %convolution_multiply_fusion = f32[32,3072]{1,0:T(8,128)} fusion(bf16[4096,32]{0,1:T(8,128)(2,1)S(1)} %convolution_convert_fusion, bf16[4096,3072]{1,0:T(8,128)(2,1)} %fusion.5), kind=kOutput, calls=%fused_computation.25 | convolution fusion | flops 805404672 | bytes 25821184 | tf_op jit(solution)/shard_map/dot_general | solution.py:121
  791.4 4.3 all-reduce.4.cloned.1.call-done
  795.6 9.9 %convolution_multiply_fusion.1 = f32[1536,32]{0,1:T(8,128)} fusion(bf16[4096,1536]{1,0:T(8,128)(2,1)} %all-gather.2.cloned.1.call-done, f32[4096,32]{0,1:T(8,128)} %all-reduce.4.cloned.1.call-done), kind=kOutput, calls=%fused_computation.28 | convolution fusion | flops 2415968256 | bytes 13303808 | tf_op jit(solution)/shard_map/dot_general | solution.py:126
  805.6 74.7 %all-reduce.6.cloned.1.call-done = (f32[1536,32]{0,1:T(8,128)}, f32[32,3072]{1,0:T(8,128)}) async-done(((f32[1536,32]{0,1:T(8,128)}, f32[32,3072]{1,0:T(8,128)}), (f32[1536,32]{0,1:T(8,128)}, f32[32,3072]{1,0:T(8,128)})) %all-reduce.6.cloned.1.call-update) | async-done | bytes 589840 | tf_op jit(solution)/shard_map/psum | solution.py:133
  (58 shorter events, 38.6 us)
Async XLA Ops:
  7.2 675.3 %copy-start = (bf16[32,3072]{1,0:T(8,128)(2,1)S(1)}, bf16[32,3072]{1,0:T(8,128)(2,1)}, u32[]{:S(2)}) copy-start(bf16[32,3072]{1,0:T(8,128)(2,1)} %param.18) | copy-start | bytes 589828
  7.2 667.0 %all-gather.2.cloned.1.call-start = ((), (), s32[]{:S(2)}) async-start(), calls=%async_computation.1 | async-start | bytes 18874368 | tf_op jit(solution)/shard_map/all_gather | solution.py:109
  40.3 5.3 copy-start.2
  45.6 4.2 copy-start.11
  167.4 17.9 %copy-start.10 = (f32[192]{0:T(256)S(1)}, f32[192]{0:T(256)}, u32[]{:S(2)}) copy-start(f32[192]{0:T(256)} %param.12) | copy-start | bytes 2308
  432.7 5.1 copy-start.1
  448.4 16.8 %copy-start.8 = (f32[1536]{0:T(1024)S(1)}, f32[1536]{0:T(1024)}, u32[]{:S(2)}) copy-start(f32[1536]{0:T(1024)} %param.14) | copy-start | bytes 18436
  448.4 16.8 %copy-start.9 = (f32[1536]{0:T(1024)S(1)}, f32[1536]{0:T(1024)}, u32[]{:S(2)}) copy-start(f32[1536]{0:T(1024)} %param.13) | copy-start | bytes 18436
  474.0 8.8 copy-start.7
  474.0 10.9 %copy-start.5 = (bf16[192,3072]{1,0:T(8,128)(2,1)S(1)}, bf16[192,3072]{1,0:T(8,128)(2,1)}, u32[]{:S(2)}) copy-start(bf16[192,3072]{1,0:T(8,128)(2,1)} %param.15) | copy-start | bytes 3538948
  482.8 312.8 %all-reduce.4.cloned.1.call-start = ((), (), s32[]{:S(2)}) async-start(), calls=%async_computation.2 | async-start | bytes 1048576 | tf_op jit(solution)/shard_map/psum | solution.py:125
  484.9 189.3 %copy-start.6 = (bf16[1536,32]{0,1:T(8,128)(2,1)S(1)}, bf16[1536,32]{0,1:T(8,128)(2,1)}, u32[]{:S(2)}) copy-start(bf16[1536,32]{0,1:T(8,128)(2,1)} %param.17) | copy-start | bytes 294916
  485.6 4.4 copy-start.3
  490.1 50.1 %collective-permute-start = (bf16[192,3072]{1,0:T(8,128)(2,1)S(1)}, bf16[192,3072]{1,0:T(8,128)(2,1)S(1)}, u32[]{:S(2)}, u32[]{:S(2)}) collective-permute-start(bf16[192,3072]{1,0:T(8,128)(2,1)S(1)} %get-tuple-element.5), channel_id=1, source_target_pairs={{0,2},{2,4},{4,6},{6,8},{8,10},{10,12},{12,14},{14,0},{1,3},{3,5},... | collective-permute-start | bytes 3538952 | tf_op jit(solution)/shard_map/ppermute | solution.py:29
  491.2 51.5 %collective-permute-start.1 = (bf16[192,3072]{1,0:T(8,128)(2,1)S(1)}, bf16[192,3072]{1,0:T(8,128)(2,1)}, u32[]{:S(2)}, u32[]{:S(2)}) collective-permute-start(bf16[192,3072]{1,0:T(8,128)(2,1)S(1)} %get-tuple-element.5), channel_id=1, source_target_pairs={{0,14},{2,0},{4,2},{6,4},{8,6},{10,8},{12,10},{14,12},{1,15},{3,1}... | collective-permute-start | bytes 3538952 | tf_op jit(solution)/shard_map/ppermute | solution.py:34
  540.2 4.7 copy-start.4
  540.2 51.8 %collective-permute-start.2 = (bf16[192,3072]{1,0:T(8,128)(2,1)S(1)}, bf16[192,3072]{1,0:T(8,128)(2,1)}, u32[]{:S(2)}, u32[]{:S(2)}) collective-permute-start(bf16[192,3072]{1,0:T(8,128)(2,1)S(1)} %collective-permute-done), channel_id=1, source_target_pairs={{0,2},{2,4},{4,6},{6,8},{8,10},{10,12},{12,14},{14,0},{1,3},{3,5},... | collective-permute-start | bytes 3538952 | tf_op jit(solution)/shard_map/ppermute | solution.py:29
  542.7 54.3 %collective-permute-start.3 = (bf16[192,3072]{1,0:T(8,128)(2,1)}, bf16[192,3072]{1,0:T(8,128)(2,1)S(1)}, u32[]{:S(2)}, u32[]{:S(2)}) collective-permute-start(bf16[192,3072]{1,0:T(8,128)(2,1)} %collective-permute-done.1), channel_id=1, source_target_pairs={{0,14},{2,0},{4,2},{6,4},{8,6},{10,8},{12,10},{14,12},{1,15},{3,1}... | collective-permute-start | bytes 3538952 | tf_op jit(solution)/shard_map/ppermute | solution.py:34
  592.0 52.4 %collective-permute-start.4 = (bf16[192,3072]{1,0:T(8,128)(2,1)}, bf16[192,3072]{1,0:T(8,128)(2,1)S(1)}, u32[]{:S(2)}, u32[]{:S(2)}) collective-permute-start(bf16[192,3072]{1,0:T(8,128)(2,1)} %collective-permute-done.2), channel_id=1, source_target_pairs={{0,2},{2,4},{4,6},{6,8},{8,10},{10,12},{12,14},{14,0},{1,3},{3,5},... | collective-permute-start | bytes 3538952 | tf_op jit(solution)/shard_map/ppermute | solution.py:29
  597.0 54.6 %collective-permute-start.5 = (bf16[192,3072]{1,0:T(8,128)(2,1)S(1)}, bf16[192,3072]{1,0:T(8,128)(2,1)S(1)}, u32[]{:S(2)}, u32[]{:S(2)}) collective-permute-start(bf16[192,3072]{1,0:T(8,128)(2,1)S(1)} %collective-permute-done.3), channel_id=1, source_target_pairs={{0,14},{2,0},{4,2},{6,4},{8,6},{10,8},{12,10},{14,12},{1,15},{3,1}... | collective-permute-start | bytes 3538952 | tf_op jit(solution)/shard_map/ppermute | solution.py:34
  644.4 28.7 %collective-permute-start.6 = (bf16[192,3072]{1,0:T(8,128)(2,1)S(1)}, bf16[192,3072]{1,0:T(8,128)(2,1)S(1)}, u32[]{:S(2)}, u32[]{:S(2)}) collective-permute-start(bf16[192,3072]{1,0:T(8,128)(2,1)S(1)} %collective-permute-done.4), channel_id=1, source_target_pairs={{0,2},{2,4},{4,6},{6,8},{8,10},{10,12},{12,14},{14,0},{1,3},{3,5},... | collective-permute-start | bytes 3538952 | tf_op jit(solution)/shard_map/ppermute | solution.py:29
  779.6 100.7 %all-reduce.6.cloned.1.call-start = ((), (), s32[]{:S(2)}) async-start(), calls=%async_computation.3 | async-start | bytes 1179648 | tf_op jit(solution)/shard_map/psum | solution.py:133
Sparse Core Ops, SparseCore 0:
  483.0 23.7 all-gather.1
  779.7 15.8 all-reduce.3
  805.7 74.5 all-reduce.5
